TPU v7x, 128 devices: a whole 4x4x4 slice. The times are simulated.
128 devices in a mesh: owner: 4 (over y), worker: 32 (over x, z, core).
Axes of the slice: x: 4, y: 4, z: 4, core: 2. Of those that a mesh axis runs over, the one named last changes fastest.
Arguments:
- states: float32 [262144, 512], P(('owner', 'worker')), may hold values from -3 to 3
- row_of_user: int32 [262144], replicated, may hold values from 0 to 262143, as said below
- event_users: int32 [65536], P(('owner', 'worker')), may hold values from 0 to 262143, as said below
- event_features: int32 [65536], P(('owner', 'worker')), may hold values from 0 to 4095
- feature_table: bfloat16 [4096, 512], replicated, may hold values from -6 to 6
- gate_in: bfloat16 [512, 1536], replicated, may hold values from -0.25 to 0.25
- gate_state: bfloat16 [512, 1536], replicated, may hold values from -0.25 to 0.25
- tower_in: bfloat16 [4096, 1024], P(('owner', 'worker')), may hold values from -0.1875 to 0.1875
- tower_out: bfloat16 [512, 4096], P(('owner', 'worker')), may hold values from -0.09375 to 0.09375
Outputs:
- new_states: float32 [262144, 512], P(('owner', 'worker'))
- scores: float32 [65536], P(('owner', 'worker'))
Inputs may be any that keep to these rules, and one draw needn't show every extreme that they name: `row_of_user`: A permutation: each user has its own state row. `event_users`: among the 512 events of one device, at most 8 have their row (row_of_user of the user) in one device's block of 2048 rows, and for every device some block receives exactly 8 of its events.
All inputs are finite; a program needn't handle non-finite values.
Results may differ from a plain program's by a relative error of at most 0.0034.
Values may be sent and summed in bfloat16 or wider, within the bound.
A program may use at most 128 MiB of HBM per device.

v0:
```python
import jax
import jax.numpy as jnp
from jax import lax
from jax.sharding import PartitionSpec as P


def gru_cell(inputs, prior, gate_in, gate_state):
    gx = jnp.dot(inputs, gate_in, preferred_element_type=jnp.float32)
    gh = jnp.dot(prior, gate_state, preferred_element_type=jnp.float32)
    width = prior.shape[-1]
    reset = jax.nn.sigmoid(gx[:, :width] + gh[:, :width])
    update = jax.nn.sigmoid(gx[:, width : 2 * width] + gh[:, width : 2 * width])
    cand = jnp.tanh(gx[:, 2 * width :] + reset * gh[:, 2 * width :])
    return (1.0 - update) * cand + update * prior.astype(jnp.float32)


def per_device(
    states,
    row_of_user,
    event_users,
    event_features,
    feature_table,
    gate_in,
    gate_state,
    tower_in,
    tower_out,
):
    shards = lax.axis_size(("owner", "worker"))
    events = event_users.shape[0]
    row_count = states.shape[0]
    width = states.shape[1]
    cap = 2 * (events // shards)
    rows = row_of_user[event_users]
    target = rows // row_count
    local = rows - target * row_count
    inputs = feature_table[event_features]
    hits = (target[:, None] == jnp.arange(shards, dtype=jnp.int32)[None, :]).astype(jnp.int32)
    rank = jnp.sum((jnp.cumsum(hits, axis=0) - hits) * hits, axis=1)
    slot = target * cap + rank
    requests = jnp.full((shards * cap,), -1, jnp.int32).at[slot].set(local).reshape(shards, cap)
    asked = lax.all_to_all(requests, ("owner", "worker"), split_axis=0, concat_axis=0, tiled=True)
    fetched = states[jnp.maximum(asked, 0)].astype(jnp.bfloat16)
    arrived, asked = (
        lax.all_to_all(fetched, ("owner", "worker"), split_axis=0, concat_axis=0, tiled=True),
        asked,
    )
    prior = arrived.reshape(shards * cap, width)[slot]
    fresh = gru_cell(inputs, prior, gate_in, gate_state)
    fresh_low = fresh.astype(jnp.bfloat16)
    delta = fresh - prior.astype(jnp.float32)
    outgoing = (
        jnp.zeros((shards * cap, width), jnp.float32)
        .at[slot]
        .set(delta)
        .reshape(shards, cap, width)
    )
    changes = lax.all_to_all(outgoing, ("owner", "worker"), split_axis=0, concat_axis=0, tiled=True)
    valid = asked.reshape(-1) >= 0
    owners_ids = jnp.where(valid, asked.reshape(-1), row_count)
    total = jax.ops.segment_sum(changes.reshape(-1, width), owners_ids, num_segments=row_count + 1)[
        :row_count
    ]
    count = jax.ops.segment_sum(valid.astype(jnp.int32), owners_ids, num_segments=row_count + 1)[
        :row_count
    ]
    new_states = states + total / jnp.maximum(count, 1).astype(jnp.float32)[:, None]
    joined = jnp.concatenate([fresh_low, inputs], axis=1)
    hidden = jax.nn.gelu(
        lax.dot_general(
            joined,
            lax.all_gather(tower_in, ("owner", "worker"), axis=0, tiled=True),
            (((1,), (1,)), ((), ())),
            preferred_element_type=jnp.float32,
        )
    ).astype(jnp.bfloat16)
    tower = lax.dot_general(
        hidden,
        lax.all_gather(tower_out, ("owner", "worker"), axis=0, tiled=True),
        (((1,), (1,)), ((), ())),
        preferred_element_type=jnp.float32,
    )
    scores = jnp.sum(tower * inputs.astype(jnp.float32), axis=1) / jnp.sqrt(jnp.float32(width))
    return (new_states, scores)


def solution(mesh):
    placed = (
        P(("owner", "worker"), None),
        P(),
        P(("owner", "worker")),
        P(("owner", "worker")),
        P(),
        P(),
        P(),
        P(("owner", "worker"), None),
        P(("owner", "worker"), None),
    )
    return jax.shard_map(
        per_device,
        mesh=mesh,
        in_specs=placed,
        out_specs=(P(("owner", "worker"), None), P(("owner", "worker"))),
        check_vma=False,
    )
```

profile of v0, /device:TPU:1, one launch (start us, length us, event | category | flops | bytes accessed | tf_op | source)
XLA Modules:
  0.0 186.0 jit_solution(2126969948334331115)
XLA Ops:
  7.2 0.0 copy-start
  7.2 0.0 all-gather.6.cloned.1.call-start
  7.2 0.7 all-gather.6.cloned.1.call-update
  7.9 0.0 all-gather.4.cloned.1.call-start
  8.0 0.7 all-gather.4.cloned.1.call-update
  8.7 0.7 compare_select_fusion.3
  9.4 6.5 %gather_fusion = s32[512]{0:T(512)S(1)} fusion(s32[262144]{0:T(1024)} %param.10, s32[1024]{0:T(1024)S(1)} %pad_clamp_fusion.2), kind=kCustom, calls=%fused_computation | custom fusion | bytes 6144 | tf_op jit(solution)/shard_map/gather | solution.py:33
  15.9 0.1 copy.15
  16.0 0.2 fusion.46
  16.3 0.2 fusion.45
  16.6 2.4 %scatter_custom_fusion = s32[1024]{0:T(1024)S(1)} fusion(s32[512]{0:T(512)S(1)} %bitcast.59, s32[512]{0:T(512)S(1)} %get-tuple-element.7, s32[]{:T(128)} %constant.17.clone.1), kind=kCustom, calls=%fused_computation.93 | custom fusion | bytes 4100 | tf_op jit(solution)/shard_map/scatter | solution.py:40
  19.0 0.1 all_to_all.12
  19.1 20.7 %all_to_all.19 = s32[128,1,8]{2,1,0:T(1,128)S(1)} all-to-all(s32[128,1,8]{2,1,0:T(1,128)S(1)} %bitcast.54), channel_id=1, replica_groups=mesh['owner'=4,'worker'=32] {'owner','worker'}, dimensions={0} | all-to-all | bytes 8192 | tf_op jit(solution)/shard_map/all_to_all | solution.py:41
  39.8 0.5 broadcast.212
  40.4 1.2 fusion.49
  41.5 0.1 reshape.170
  41.6 0.0 copy-start.4
  41.7 7.3 %gather_fusion.2 = bf16[1024,512]{1,0:T(8,128)(2,1)} fusion(f32[2048,512]{1,0:T(8,128)} %param.9, s32[1024]{0:T(1024)S(1)} %broadcast_clamp_fusion), kind=kCustom, calls=%fused_computation.2 | custom fusion | bytes 2101248 | tf_op jit(solution)/shard_map/gather | solution.py:42
  49.0 4.6 %all-to-all-start.1 = ((bf16[128,8,512]{2,1,0:T(8,128)(2,1)}), bf16[128,8,512]{2,1,0:T(8,128)(2,1)S(1)}, u32[]{:S(2)}, u32[]{:S(2)}) async-start(bf16[128,8,512]{2,1,0:T(8,128)(2,1)} %bitcast.51), calls=%async_computation.1 | async-start | bytes 2097152 | tf_op jit(solution)/shard_map/all_to_all | solution.py:44
  53.6 0.0 copy-done.4
  53.6 4.7 %gather_fusion.1 = bf16[512,512]{1,0:T(8,128)(2,1)S(1)} fusion(bf16[4096,512]{1,0:T(8,128)(2,1)} %param.13, s32[1024]{0:T(1024)S(1)} %pad_clamp_fusion.1), kind=kCustom, calls=%fused_computation.1 | custom fusion | bytes 1050624 | tf_op jit(solution)/shard_map/gather | solution.py:36
  58.3 0.0 copy-start.2
  58.4 0.0 copy-done
  58.4 2.6 %fusion.68 = f32[512,1536]{1,0:T(8,128)} fusion(bf16[512,512]{1,0:T(8,128)(2,1)S(1)} %gather_fusion.1, bf16[512,1536]{1,0:T(8,128)(2,1)S(1)} %copy-done), kind=kOutput, calls=%fused_computation.104 | convolution fusion | flops 805306368 | bytes 5242880 | tf_op jit(solution)/shard_map/dot_general | solution.py:8
  61.0 11.9 %all-to-all-done.1 = bf16[128,8,512]{2,1,0:T(8,128)(2,1)S(1)} async-done(((bf16[128,8,512]{2,1,0:T(8,128)(2,1)}), bf16[128,8,512]{2,1,0:T(8,128)(2,1)S(1)}, u32[]{:S(2)}, u32[]{:S(2)}) %all-to-all-start.1) | async-done | bytes 1048608 | tf_op jit(solution)/shard_map/all_to_all | solution.py:44
  72.9 0.0 copy-done.2
  72.9 2.0 %gather_fusion.3 = bf16[512,512]{1,0:T(8,128)(2,1)S(1)} fusion(bf16[1024,512]{1,0:T(8,128)(2,1)S(1)} %bitcast.49, s32[1024]{0:T(1024)S(1)} %pad_clamp_fusion), kind=kCustom, calls=%fused_computation.3 | custom fusion | bytes 1050624 | tf_op jit(solution)/shard_map/gather | solution.py:47
  74.9 0.0 copy-start.1
  74.9 2.6 %fusion.69 = f32[512,1536]{1,0:T(8,128)S(1)} fusion(bf16[512,512]{1,0:T(8,128)(2,1)S(1)} %gather_fusion.3, bf16[512,1536]{1,0:T(8,128)(2,1)} %param.15), kind=kOutput, calls=%fused_computation.105 | convolution fusion | flops 805306368 | bytes 5242880 | tf_op jit(solution)/shard_map/dot_general | solution.py:9
  77.5 0.0 copy-done.1
  77.5 1.9 %fusion.66 = (bf16[512,512]{1,0:T(8,128)(2,1)S(1)}, f32[512,512]{1,0:T(8,128)}) fusion(bf16[512,512]{1,0:T(8,128)(2,1)S(1)} %gather_fusion.3, f32[512,1536]{1,0:T(8,128)S(1)} %fusion.69, f32[512,1536]{1,0:T(8,128)S(1)} %copy-done.1), kind=kLoop, calls=%fused_computation.103 | loop fusion | flops 4194304 | bytes 8388608 | tf_op jit(solution)/shard_map/convert_element_type | solution.py:49
  79.4 0.0 copy-start.3
  79.4 4.4 %scatter_custom_fusion.1 = f32[1024,512]{1,0:T(8,128)} fusion(s32[512]{0:T(512)S(1)} %bitcast.61, f32[512,512]{1,0:T(8,128)} %get-tuple-element.6, bf16[512,512]{1,0:T(8,128)(2,1)S(1)} %gather_fusion.3, f32[]{:T(128)} %constant.16.clone.1), kind=kCustom, calls=%fused_computation.28 | custom fusion | flops 524288 | bytes 3670020 | tf_op jit(solution)/shard_map/scatter | solution.py:54
  83.8 5.7 %all-to-all-start.2 = ((f32[128,8,512]{2,1,0:T(8,128)}), f32[128,8,512]{2,1,0:T(8,128)}, u32[]{:S(2)}, u32[]{:S(2)}) async-start(f32[128,8,512]{2,1,0:T(8,128)} %bitcast.50), calls=%async_computation.2 | async-start | bytes 4194304 | tf_op jit(solution)/shard_map/all_to_all | solution.py:57
  89.5 0.0 copy-done.3
  89.5 0.2 copy.18
  89.7 0.1 reshape.147
  89.8 0.1 reshape.212
  89.9 6.8 %scatter_custom_fusion.3 = s32[2049]{0:T(1024)S(1)} fusion(s32[1024]{0:T(1024)S(1)} %bitcast.62, s32[1024]{0:T(1024)S(1)} %reshape.212, s32[]{:T(128)} %constant.18.clone.1), kind=kCustom, calls=%fused_computation.66 | custom fusion | flops 1024 | bytes 8200 | tf_op jit(solution)/shard_map/scatter-add | solution.py:63
  96.7 23.3 %all-to-all-done.2 = f32[128,8,512]{2,1,0:T(8,128)} async-done(((f32[128,8,512]{2,1,0:T(8,128)}), f32[128,8,512]{2,1,0:T(8,128)}, u32[]{:S(2)}, u32[]{:S(2)}) %all-to-all-start.2) | async-done | bytes 2097184 | tf_op jit(solution)/shard_map/all_to_all | solution.py:57
  120.0 9.8 %scatter_custom_fusion.2 = f32[2049,512]{1,0:T(8,128)} fusion(s32[1024]{0:T(1024)S(1)} %bitcast.63, f32[]{:T(128)} %constant.16.clone.1, f32[128,8,512]{2,1,0:T(8,128)} %all-to-all-done.2), kind=kCustom, calls=%fused_computation.20 | custom fusion | flops 524288 | bytes 6293508 | tf_op jit(solution)/shard_map/scatter-add | solution.py:60
  129.8 6.1 %fusion.8 = f32[2048,512]{1,0:T(8,128)} fusion(f32[2048,512]{1,0:T(8,128)} %param.9, f32[2049,512]{1,0:T(8,128)} %scatter_custom_fusion.2, f32[2048]{0:T(1024)S(1)} %fusion.50), kind=kLoop, calls=%fused_computation.18 | loop fusion | flops 2097152 | bytes 12591104 | tf_op jit(solution)/shard_map/add | solution.py:66
  135.9 0.0 all-gather.6.cloned.1.call-done
  135.9 6.9 %reshape.222 = bf16[512,4096]{1,0:T(8,128)(2,1)} reshape(bf16[128,4,4096]{2,1,0:T(4,128)(2,1)} %all-gather.6.cloned.1.call-done) | data formatting | bytes 8388608
  142.8 24.3 %all-gather.4.cloned.1.call-done = bf16[4096,1024]{1,0:T(8,128)(2,1)} async-done(((bf16[32,1024]{1,0:T(8,128)(2,1)}), bf16[4096,1024]{1,0:T(8,128)(2,1)}) %all-gather.4.cloned.1.call-update) | async-done | bytes 8388624 | tf_op jit(solution)/shard_map/all_gather | solution.py:71
  167.1 11.4 %fusion.17 = f32[512]{0:T(512)S(1)} fusion(bf16[512,4096]{1,0:T(8,128)(2,1)} %reshape.222, bf16[4096,1024]{1,0:T(8,128)(2,1)} %all-gather.4.cloned.1.call-done, bf16[512,512]{1,0:T(8,128)(2,1)S(1)} %copy-done.3, bf16[512,512]{1,0:T(8,128)(2,1)S(1)} %get-tuple-element.5, bf16[512,512]{0,1:T(8,128)(2,1)S(1)} %copy.18), kind=kOutput, calls=%fused_computation.26 | convolution fusion | flops 6464208384 | bytes 14157824 | tf_op jit(solution)/shard_map/dot_general | solution.py:76
  178.6 0.6 broadcast_multiply_fusion
  (16 shorter events, 0.2 us)
Async XLA Ops:
  7.2 51.2 %copy-start = (bf16[512,1536]{1,0:T(8,128)(2,1)S(1)}, bf16[512,1536]{1,0:T(8,128)(2,1)}, u32[]{:S(2)}) copy-start(bf16[512,1536]{1,0:T(8,128)(2,1)} %param.14) | copy-start | bytes 4718596
  7.2 128.7 %all-gather.6.cloned.1.call-start = ((), (), s32[]{:S(2)}) async-start(), calls=%async_computation.4 | async-start | bytes 4227072 | tf_op jit(solution)/shard_map/all_gather | solution.py:78
  7.9 159.2 %all-gather.4.cloned.1.call-start = ((), (), s32[]{:S(2)}) async-start(), calls=%async_computation.3 | async-start | bytes 8454144 | tf_op jit(solution)/shard_map/all_gather | solution.py:71
  41.6 11.9 %copy-start.4 = (s32[512]{0:T(512)S(1)}, s32[512]{0:T(512)}, u32[]{:S(2)}) copy-start(s32[512]{0:T(512)} %param.12) | copy-start | bytes 6148
  49.0 24.0 %all-to-all-start.1 = ((bf16[128,8,512]{2,1,0:T(8,128)(2,1)}), bf16[128,8,512]{2,1,0:T(8,128)(2,1)S(1)}, u32[]{:S(2)}, u32[]{:S(2)}) async-start(bf16[128,8,512]{2,1,0:T(8,128)(2,1)} %bitcast.51), calls=%async_computation.1 | async-start | bytes 2097152 | tf_op jit(solution)/shard_map/all_to_all | solution.py:44
  58.3 14.6 %copy-start.2 = (bf16[512,512]{1,0:T(8,128)(2,1)}, bf16[512,512]{1,0:T(8,128)(2,1)S(1)}, u32[]{:S(2)}) copy-start(bf16[512,512]{1,0:T(8,128)(2,1)S(1)} %gather_fusion.1) | copy-start | bytes 1572868
  74.9 2.6 %copy-start.1 = (f32[512,1536]{1,0:T(8,128)S(1)}, f32[512,1536]{1,0:T(8,128)}, u32[]{:S(2)}) copy-start(f32[512,1536]{1,0:T(8,128)} %fusion.68) | copy-start | bytes 9437188
  79.4 10.1 %copy-start.3 = (bf16[512,512]{1,0:T(8,128)(2,1)S(1)}, bf16[512,512]{1,0:T(8,128)(2,1)}, u32[]{:S(2)}) copy-start(bf16[512,512]{1,0:T(8,128)(2,1)} %copy-done.2) | copy-start | bytes 1572868
  83.8 36.2 %all-to-all-start.2 = ((f32[128,8,512]{2,1,0:T(8,128)}), f32[128,8,512]{2,1,0:T(8,128)}, u32[]{:S(2)}, u32[]{:S(2)}) async-start(f32[128,8,512]{2,1,0:T(8,128)} %bitcast.50), calls=%async_computation.2 | async-start | bytes 4194304 | tf_op jit(solution)/shard_map/all_to_all | solution.py:57
Sparse Core Ops, SparseCore 0:
  11.2 73.3 all-gather.5
  87.6 79.5 all-gather.3
where the time goes:
time: 187 us; the launch traced here: 186 us
  waiting for transfers between devices  60.9 us (33%)
  other arithmetic  32 us (17%)
  local copies, waits for them, and re-layouts  31.1 us (17%)
  blocking collectives  20.7 us (11%)
  matrix products  16.6 us (9%)
  between operations  14.3 us (8%)
  starting transfers between devices  10.3 us (6%)
    all_gather x1, waiting for transfers between devices, per_device(): lax.all_gather(tower_in, ('owner', 'worker'), axis=0, tiled=True)  24.3 us
    all_to_all x1, waiting for transfers between devices, per_device(): lax.all_to_all(outgoing, ('owner', 'worker'), split_axis=0, concat_axis=0...  23.3 us
    all_to_all x1, blocking collectives, per_device(): lax.all_to_all(requests, ('owner', 'worker'), split_axis=0, concat_axis=0...  20.7 us
    all_to_all x1, waiting for transfers between devices, per_device(): lax.all_to_all(fetched, ('owner', 'worker'), split_axis=0, concat_axis=0,...  11.9 us
    dot_general x1, matrix products, per_device(): lax.dot_general(hidden, lax.all_gather(tower_out, ('owner', 'worker'), ax...  11.4 us
    scatter-add x1, other arithmetic, per_device(): jax.ops.segment_sum(changes.reshape(-1, width), owners_ids, num_segments=...  9.8 us
    gather x1, local copies, waits for them, and re-layouts, per_device(): fetched = states[jnp.maximum(asked, 0)].astype(jnp.bfloat16)  7.29 us
    unnamed x12, local copies, waits for them, and re-layouts  6.97 us
  transfers between devices with their start and end apart: 4, of which 3 were waited for; matrix products, arithmetic and copies ran while one was open for 36% of the time, Pallas kernels for 0%

commit v1 on v0

--- a/solution.py
+++ b/solution.py
@@ -65,10 +65,19 @@
     ]
     new_states = states + total / jnp.maximum(count, 1).astype(jnp.float32)[:, None]
     joined = jnp.concatenate([fresh_low, inputs], axis=1)
+    _prepare_tasks = lambda xs: jnp.concatenate(
+        jax.lax.all_to_all(
+            jnp.stack([xs for _ in range(jax.lax.axis_size(("owner", "worker")))], axis=0),
+            ("owner", "worker"),
+            split_axis=0,
+            concat_axis=0,
+        ),
+        0,
+    )
     hidden = jax.nn.gelu(
         lax.dot_general(
             joined,
-            lax.all_gather(tower_in, ("owner", "worker"), axis=0, tiled=True),
+            _prepare_tasks(tower_in),
             (((1,), (1,)), ((), ())),
             preferred_element_type=jnp.float32,
         )

time: 187 us -> 274 us (1.47)
  waiting for transfers between devices: 60.9 us -> 139 us
  starting transfers between devices: 10.3 us -> 16.6 us
  local copies, waits for them, and re-layouts: 31.1 us -> 35.4 us
    all_gather x1, waiting for transfers between devices: 0.01 us -> 97.1 us  [per_device(): lax.all_gather(tower_out, ('owner', 'worker'), axis=0, tiled=True)]
    all_gather x1 -> x0, waiting for transfers between devices: 24.3 us -> none  [per_device(): lax.all_gather(tower_in, ('owner', 'worker'), axis=0, tiled=True)]
    all_to_all x1, waiting for transfers between devices: 23.3 us -> 29.4 us  [per_device(): lax.all_to_all(outgoing, ('owner', 'worker'), split_axis=0, concat_axis=0...]
    all_to_all x0 -> x1, starting transfers between devices: none -> 6.04 us  [per_device(): jax.lax.all_to_all(jnp.stack([xs for _ in range(jax.lax.axis_size(('owner...]
    another operation x3 -> x4, local copies, waits for them, and re-layouts: 0.03 us -> 4.31 us  [the longest x1 4.28 us: per_device(): jnp.stack([xs for _ in range(jax.lax.axis_size(('owner', 'worker')))], ax...]
    unnamed x12 -> x16, local copies, waits for them, and re-layouts: 6.97 us -> 6.96 us
  transfers between devices with their start and end apart: 4 -> 4, of which waited for: 3 -> 3; matrix products, arithmetic and copies ran while one was open for 36% -> 15% of each run, Pallas kernels for 0% -> 0%
where the time goes in v1:
time: 274 us; the launch traced here: 273 us
  waiting for transfers between devices  139 us (51%)
  local copies, waits for them, and re-layouts  35.4 us (13%)
  other arithmetic  31 us (11%)
  blocking collectives  20.7 us (8%)
  starting transfers between devices  16.6 us (6%)
  matrix products  16.6 us (6%)
  between operations  14.3 us (5%)
    all_gather x1, waiting for transfers between devices, per_device(): lax.all_gather(tower_out, ('owner', 'worker'), axis=0, tiled=True)  97.1 us
    all_to_all x1, waiting for transfers between devices, per_device(): lax.all_to_all(outgoing, ('owner', 'worker'), split_axis=0, concat_axis=0...  29.4 us
    all_to_all x1, blocking collectives, per_device(): lax.all_to_all(requests, ('owner', 'worker'), split_axis=0, concat_axis=0...  20.7 us
    all_to_all x1, waiting for transfers between devices, per_device(): lax.all_to_all(fetched, ('owner', 'worker'), split_axis=0, concat_axis=0,...  11.9 us
    dot_general x1, matrix products, per_device(): lax.dot_general(hidden, lax.all_gather(tower_out, ('owner', 'worker'), ax...  11.4 us
    scatter-add x1, other arithmetic, per_device(): jax.ops.segment_sum(changes.reshape(-1, width), owners_ids, num_segments=...  9.77 us
    gather x1, local copies, waits for them, and re-layouts, per_device(): fetched = states[jnp.maximum(asked, 0)].astype(jnp.bfloat16)  7.3 us
    unnamed x16, local copies, waits for them, and re-layouts  6.96 us
  transfers between devices with their start and end apart: 4, of which 3 were waited for; matrix products, arithmetic and copies ran while one was open for 15% of the time, Pallas kernels for 0%

profile of v1, /device:TPU:1, one launch (start us, length us, event | category | flops | bytes accessed | tf_op | source)
XLA Modules:
  0.0 273.5 jit_solution(6361044122485502325)
XLA Ops:
  7.2 0.0 copy-start
  7.2 0.8 compare_select_fusion.3
  8.0 6.5 %gather_fusion = s32[512]{0:T(512)S(1)} fusion(s32[262144]{0:T(1024)} %param.10, s32[1024]{0:T(1024)S(1)} %pad_clamp_fusion.2), kind=kCustom, calls=%fused_computation | custom fusion | bytes 6144 | tf_op jit(solution)/shard_map/gather | solution.py:33
  14.5 0.1 copy.15
  14.6 0.2 fusion.46
  15.0 0.2 fusion.45
  15.2 2.4 scatter_custom_fusion
  17.7 0.1 all_to_all.15
  17.8 20.7 %all_to_all.24 = s32[128,1,8]{2,1,0:T(1,128)S(1)} all-to-all(s32[128,1,8]{2,1,0:T(1,128)S(1)} %bitcast.55), channel_id=1, replica_groups=mesh['owner'=4,'worker'=32] {'owner','worker'}, dimensions={0} | all-to-all | bytes 8192 | tf_op jit(solution)/shard_map/all_to_all | solution.py:41
  38.5 0.5 broadcast.214
  39.0 1.2 fusion.49
  40.2 0.1 reshape.176
  40.3 0.0 copy-start.6
  40.3 7.3 %gather_fusion.2 = bf16[1024,512]{1,0:T(8,128)(2,1)} fusion(f32[2048,512]{1,0:T(8,128)} %param.9, s32[1024]{0:T(1024)S(1)} %broadcast_clamp_fusion), kind=kCustom, calls=%fused_computation.2 | custom fusion | bytes 2101248 | tf_op jit(solution)/shard_map/gather | solution.py:42
  47.6 4.6 %all-to-all-start.1 = ((bf16[128,8,512]{2,1,0:T(8,128)(2,1)}), bf16[128,8,512]{2,1,0:T(8,128)(2,1)S(1)}, u32[]{:S(2)}, u32[]{:S(2)}) async-start(bf16[128,8,512]{2,1,0:T(8,128)(2,1)} %bitcast.52), calls=%async_computation.1 | async-start | bytes 2097152 | tf_op jit(solution)/shard_map/all_to_all | solution.py:44
  52.2 0.0 copy-done.6
  52.2 4.7 %gather_fusion.1 = bf16[512,512]{1,0:T(8,128)(2,1)S(1)} fusion(bf16[4096,512]{1,0:T(8,128)(2,1)} %param.13, s32[1024]{0:T(1024)S(1)} %pad_clamp_fusion.1), kind=kCustom, calls=%fused_computation.1 | custom fusion | bytes 1050624 | tf_op jit(solution)/shard_map/gather | solution.py:36
  57.0 0.0 copy-start.2
  57.0 0.0 copy-done
  57.0 2.6 fusion.68
  59.6 11.9 %all-to-all-done.1 = bf16[128,8,512]{2,1,0:T(8,128)(2,1)S(1)} async-done(((bf16[128,8,512]{2,1,0:T(8,128)(2,1)}), bf16[128,8,512]{2,1,0:T(8,128)(2,1)S(1)}, u32[]{:S(2)}, u32[]{:S(2)}) %all-to-all-start.1) | async-done | bytes 1048608 | tf_op jit(solution)/shard_map/all_to_all | solution.py:44
  71.5 0.0 copy-done.2
  71.5 2.0 gather_fusion.3
  73.5 0.0 copy-start.1
  73.5 2.5 fusion.69
  76.0 0.0 copy-done.1
  76.0 1.7 fusion.66
  77.7 3.7 %scatter_custom_fusion.1 = f32[1024,512]{1,0:T(8,128)} fusion(s32[512]{0:T(512)S(1)} %bitcast.62, f32[512,512]{1,0:T(8,128)S(1)} %get-tuple-element.6, bf16[512,512]{1,0:T(8,128)(2,1)S(1)} %gather_fusion.3, f32[]{:T(128)} %constant.16.clone.1), kind=kCustom, calls=%fused_computation.28 | custom fusion | flops 524288 | bytes 3670020 | tf_op jit(solution)/shard_map/scatter | solution.py:54
  81.4 5.7 %all-to-all-start.2 = ((f32[128,8,512]{2,1,0:T(8,128)}), f32[128,8,512]{2,1,0:T(8,128)}, u32[]{:S(2)}, u32[]{:S(2)}) async-start(f32[128,8,512]{2,1,0:T(8,128)} %bitcast.51), calls=%async_computation.2 | async-start | bytes 4194304 | tf_op jit(solution)/shard_map/all_to_all | solution.py:57
  87.1 0.2 all-gather.3.cloned.1.call-start
  87.4 0.5 all-gather.3.cloned.1.call-update
  87.9 29.4 %all-to-all-done.2 = f32[128,8,512]{2,1,0:T(8,128)} async-done(((f32[128,8,512]{2,1,0:T(8,128)}), f32[128,8,512]{2,1,0:T(8,128)}, u32[]{:S(2)}, u32[]{:S(2)}) %all-to-all-start.2) | async-done | bytes 2097184 | tf_op jit(solution)/shard_map/all_to_all | solution.py:57
  117.3 0.0 copy-done.5
  117.3 4.3 %stack.2 = bf16[128,32,1024]{2,1,0:T(8,128)(2,1)} broadcast(bf16[32,1024]{1,0:T(8,128)(2,1)S(1)} %copy-done.5), dimensions={1,2} | broadcast | bytes 8454144 | tf_op jit(solution)/shard_map/stack | solution.py:70
  121.6 6.0 %all-to-all-start.3 = ((bf16[128,32,1024]{2,1,0:T(8,128)(2,1)}), bf16[128,32,1024]{2,1,0:T(8,128)(2,1)}, u32[]{:S(2)}, u32[]{:S(2)}) async-start(bf16[128,32,1024]{2,1,0:T(8,128)(2,1)} %stack.2), calls=%async_computation.3 | async-start | bytes 16777216 | tf_op jit(solution)/shard_map/all_to_all | solution.py:69
  127.7 0.0 copy-done.3
  127.7 0.2 copy.18
  127.9 0.1 reshape.152
  128.0 0.1 reshape.218
  128.1 6.8 %scatter_custom_fusion.3 = s32[2049]{0:T(1024)S(1)} fusion(s32[1024]{0:T(1024)S(1)} %bitcast.63, s32[1024]{0:T(1024)S(1)} %reshape.218, s32[]{:T(128)} %constant.18.clone.1), kind=kCustom, calls=%fused_computation.66 | custom fusion | flops 1024 | bytes 8200 | tf_op jit(solution)/shard_map/scatter-add | solution.py:63
  134.9 9.8 %scatter_custom_fusion.2 = f32[2049,512]{1,0:T(8,128)} fusion(s32[1024]{0:T(1024)S(1)} %bitcast.64, f32[]{:T(128)} %constant.16.clone.1, f32[128,8,512]{2,1,0:T(8,128)} %all-to-all-done.2), kind=kCustom, calls=%fused_computation.20 | custom fusion | flops 524288 | bytes 6293508 | tf_op jit(solution)/shard_map/scatter-add | solution.py:60
  144.6 6.0 %fusion.8 = f32[2048,512]{1,0:T(8,128)} fusion(f32[2048,512]{1,0:T(8,128)} %param.9, f32[2049,512]{1,0:T(8,128)} %scatter_custom_fusion.2, f32[2048]{0:T(1024)S(1)} %fusion.50), kind=kLoop, calls=%fused_computation.18 | loop fusion | flops 2097152 | bytes 12591104 | tf_op jit(solution)/shard_map/add | solution.py:66
  150.6 97.1 %all-gather.3.cloned.1.call-done = bf16[128,4,4096]{2,1,0:T(4,128)(2,1)} async-done(((bf16[1,4,4096]{2,1,0:T(4,128)(2,1)}), bf16[128,4,4096]{2,1,0:T(4,128)(2,1)}) %all-gather.3.cloned.1.call-update) | async-done | bytes 4194320 | tf_op jit(solution)/shard_map/all_gather | solution.py:87
  247.7 6.9 %reshape.228 = bf16[512,4096]{1,0:T(8,128)(2,1)} reshape(bf16[128,4,4096]{2,1,0:T(4,128)(2,1)} %all-gather.3.cloned.1.call-done) | data formatting | bytes 8388608
  254.6 0.0 all-to-all-done.3
  254.6 0.0 copy-done.4
  254.6 11.4 %fusion.17 = f32[512]{0:T(512)S(1)} fusion(bf16[512,4096]{1,0:T(8,128)(2,1)} %reshape.228, bf16[4096,1024]{1,0:T(8,128)(2,1)} %bitcast.13, bf16[512,512]{1,0:T(8,128)(2,1)S(1)} %copy-done.3, bf16[512,512]{1,0:T(8,128)(2,1)S(1)} %copy-done.4, bf16[512,512]{0,1:T(8,128)(2,1)S(1)} %copy.18), kind=kOutput, calls=%fused_computation.26 | convolution fusion | flops 6464208384 | bytes 14157824 | tf_op jit(solution)/shard_map/dot_general | solution.py:85
  266.0 0.6 broadcast_multiply_fusion
  (19 shorter events, 0.2 us)
Async XLA Ops:
  7.2 49.8 %copy-start = (bf16[512,1536]{1,0:T(8,128)(2,1)S(1)}, bf16[512,1536]{1,0:T(8,128)(2,1)}, u32[]{:S(2)}) copy-start(bf16[512,1536]{1,0:T(8,128)(2,1)} %param.14) | copy-start | bytes 4718596
  40.3 11.9 %copy-start.6 = (s32[512]{0:T(512)S(1)}, s32[512]{0:T(512)}, u32[]{:S(2)}) copy-start(s32[512]{0:T(512)} %param.12) | copy-start | bytes 6148
  47.6 23.9 %all-to-all-start.1 = ((bf16[128,8,512]{2,1,0:T(8,128)(2,1)}), bf16[128,8,512]{2,1,0:T(8,128)(2,1)S(1)}, u32[]{:S(2)}, u32[]{:S(2)}) async-start(bf16[128,8,512]{2,1,0:T(8,128)(2,1)} %bitcast.52), calls=%async_computation.1 | async-start | bytes 2097152 | tf_op jit(solution)/shard_map/all_to_all | solution.py:44
  57.0 14.5 %copy-start.2 = (bf16[512,512]{1,0:T(8,128)(2,1)}, bf16[512,512]{1,0:T(8,128)(2,1)S(1)}, u32[]{:S(2)}) copy-start(bf16[512,512]{1,0:T(8,128)(2,1)S(1)} %gather_fusion.1) | copy-start | bytes 1572868
  73.5 2.6 copy-start.1
  77.7 39.6 %copy-start.5 = (bf16[32,1024]{1,0:T(8,128)(2,1)S(1)}, bf16[32,1024]{1,0:T(8,128)(2,1)}, u32[]{:S(2)}) copy-start(bf16[32,1024]{1,0:T(8,128)(2,1)} %param.16) | copy-start | bytes 196612
  81.4 35.9 %all-to-all-start.2 = ((f32[128,8,512]{2,1,0:T(8,128)}), f32[128,8,512]{2,1,0:T(8,128)}, u32[]{:S(2)}, u32[]{:S(2)}) async-start(f32[128,8,512]{2,1,0:T(8,128)} %bitcast.51), calls=%async_computation.2 | async-start | bytes 4194304 | tf_op jit(solution)/shard_map/all_to_all | solution.py:57
  87.1 160.5 %all-gather.3.cloned.1.call-start = ((), (), s32[]{:S(2)}) async-start(), calls=%async_computation.4 | async-start | bytes 4227072 | tf_op jit(solution)/shard_map/all_gather | solution.py:87
  121.6 6.1 %copy-start.3 = (bf16[512,512]{1,0:T(8,128)(2,1)S(1)}, bf16[512,512]{1,0:T(8,128)(2,1)}, u32[]{:S(2)}) copy-start(bf16[512,512]{1,0:T(8,128)(2,1)} %copy-done.2) | copy-start | bytes 1572868
  121.6 133.0 %all-to-all-start.3 = ((bf16[128,32,1024]{2,1,0:T(8,128)(2,1)}), bf16[128,32,1024]{2,1,0:T(8,128)(2,1)}, u32[]{:S(2)}, u32[]{:S(2)}) async-start(bf16[128,32,1024]{2,1,0:T(8,128)(2,1)} %stack.2), calls=%async_computation.3 | async-start | bytes 16777216 | tf_op jit(solution)/shard_map/all_to_all | solution.py:69
  150.6 104.0 %copy-start.4 = (bf16[512,512]{1,0:T(8,128)(2,1)S(1)}, bf16[512,512]{1,0:T(8,128)(2,1)}, u32[]{:S(2)}) copy-start(bf16[512,512]{1,0:T(8,128)(2,1)} %get-tuple-element.5) | copy-start | bytes 1572868
Sparse Core Ops, SparseCore 0:
  91.1 156.4 all-gather.2
